TPU v7x, 128 devices: a whole 4x4x4 slice. The times are simulated.
128 devices in a mesh: frame: 32 (over x, y, z_lo), row: 4 (over z_hi, core).
Axes of the slice: x: 4, y: 4, z: 4 (z_hi: 2, z_lo: 2; z = z_hi * 2 + z_lo), core: 2. Of those that a mesh axis runs over, the one named last changes fastest.
Arguments:
- query_pre: bfloat16 [2240, 32, 16, 128], P(None, 'frame', 'row'), may hold values from -6 to 6
- key_pre: bfloat16 [2240, 32, 16, 128], P(None, 'frame', 'row'), may hold values from -80 to 80
- values: bfloat16 [2240, 32, 16, 128], P(None, 'frame', 'row'), may hold values from -1 to 2
- cotangent: bfloat16 [2240, 32, 16, 128], P(None, 'frame', 'row'), may hold values from -3072 to 3072
- kernel: bfloat16 [3, 3, 2240], replicated, may hold values from -0.29882812 to 0.59765625
Outputs:
- grad_query: bfloat16 [2240, 32, 16, 128], P(None, 'frame', 'row')
- grad_key: bfloat16 [2240, 32, 16, 128], P(None, 'frame', 'row')
- grad_values: bfloat16 [2240, 32, 16, 128], P(None, 'frame', 'row')
All inputs are finite; a program needn't handle non-finite values.
Results may differ from a plain program's by a relative error of at most 0.008.
Values may be sent and summed in bfloat16 or wider, within the bound.
A program may use at most 128 MiB of HBM per device.

v0:
```python
import jax
import jax.numpy as jnp
from jax import lax
from jax.sharding import PartitionSpec as P

HD = 32
denominator_eps = 0.001


def extended(array, sides, width):
    for axis, dim in sides:
        size, length = (lax.axis_size(axis), array.shape[dim])
        up = [(i, (i + 1) % size) for i in range(size - 1)]
        down = [(j, i) for i, j in up]
        last = lax.slice_in_dim(array, length - width, length, axis=dim)
        leading = lax.slice_in_dim(array, 0, width, axis=dim)
        before = lax.ppermute(last, axis, up)
        after = lax.ppermute(leading, axis, down)
        array = jnp.concatenate([before, array, after], axis=dim)
    return array


def conv_taps(padded, weights, flipped, row_count, col_count):
    summed = None
    for tap_row in range(3):
        for tap_col in range(3):
            start_row = 2 - tap_row if flipped else tap_row
            start_col = 2 - tap_col if flipped else tap_col
            window = padded[
                :, :, start_row : start_row + row_count, start_col : start_col + col_count
            ]
            tap_term = weights[tap_row, tap_col][:, None, None, None] * window
            summed = tap_term if summed is None else summed + tap_term
    return summed


def pad_columns(field):
    return jnp.pad(field, ((0, 0), (0, 0), (0, 0), (1, 1)))


def shards(query_pre, key_pre, values, cotangent, kernel):
    highest = lax.Precision.HIGHEST
    channels, frames, row_count, col_count = values.shape
    head_count = channels // HD
    tokens_dev = frames * row_count * col_count
    all_tokens = tokens_dev * lax.axis_size("frame") * lax.axis_size("row")
    flat = (head_count, HD, tokens_dev)
    weights = kernel.astype(jnp.float32)
    value_ext = extended(values, (("row", 2),), 1)
    value_pad = pad_columns(value_ext.astype(jnp.float32))
    mixed = conv_taps(value_pad, weights, False, row_count, col_count).reshape(flat)
    key_act = jax.nn.relu(key_pre.astype(jnp.float32)).reshape(flat)
    query_act = jax.nn.relu(query_pre.astype(jnp.float32)).reshape(flat)
    local_state = jnp.einsum("hjt,het->hje", key_act, mixed, precision=highest)
    local_sum = jnp.sum(key_act, axis=2)
    state, key_sum = lax.psum((local_state, local_sum), ("frame", "row"))
    denom = (
        jnp.einsum("hj,hjt->ht", key_sum, query_act, precision=highest)
        + denominator_eps * all_tokens
    )
    numer = jnp.einsum("hje,hjt->het", state, query_act, precision=highest)
    output = numer / denom[:, None, :]
    grad_out = cotangent.astype(jnp.float32).reshape(flat)
    grad_num = grad_out / denom[:, None, :]
    grad_den = -jnp.sum(grad_out * output, axis=1) / denom
    local_gstate = jnp.einsum("hjt,het->hje", query_act, grad_num, precision=highest)
    local_gsum = jnp.einsum("hjt,ht->hj", query_act, grad_den, precision=highest)
    grad_state, grad_sum = lax.psum((local_gstate, local_gsum), ("frame", "row"))
    grad_qact = (
        jnp.einsum("hje,het->hjt", state, grad_num, precision=highest)
        + key_sum[:, :, None] * grad_den[:, None, :]
    )
    grad_query = (
        jnp.where(query_pre.reshape(flat) > 0, grad_qact, 0.0)
        .astype(jnp.bfloat16)
        .reshape(values.shape)
    )
    grad_mixed = jnp.einsum("hje,hjt->het", grad_state, key_act, precision=highest)
    grad_kact = (
        jnp.einsum("hje,het->hjt", grad_state, mixed, precision=highest) + grad_sum[:, :, None]
    )
    grad_key = (
        jnp.where(key_pre.reshape(flat) > 0, grad_kact, 0.0)
        .astype(jnp.bfloat16)
        .reshape(values.shape)
    )
    grad_grid = grad_mixed.reshape(channels, frames, row_count, col_count)
    grad_ext = extended(grad_grid.astype(jnp.bfloat16), (("row", 2),), 1).astype(grad_grid.dtype)
    grad_values = conv_taps(pad_columns(grad_ext), weights, True, row_count, col_count).astype(
        jnp.bfloat16
    )
    return (grad_query, grad_key, grad_values)


def solution(mesh):
    return jax.shard_map(
        shards,
        mesh=mesh,
        in_specs=(
            P(None, "frame", "row", None),
            P(None, "frame", "row", None),
            P(None, "frame", "row", None),
            P(None, "frame", "row", None),
            P(),
        ),
        out_specs=(
            P(None, "frame", "row", None),
            P(None, "frame", "row", None),
            P(None, "frame", "row", None),
        ),
        check_vma=False,
    )
```

profile of v0, /device:TPU:1, one launch (start us, length us, event | category | flops | bytes accessed | tf_op | source)
XLA Modules:
  0.0 554.9 jit_solution(3331773693273662485)
XLA Ops:
  7.2 0.0 all-reduce.5.cloned.1.call-start
  7.2 4.5 fusion.36
  11.7 0.9 copy.42
  12.6 3.4 collective-permute-start.1
  16.0 0.9 copy.41
  16.9 5.5 collective-permute-start
  22.4 5.1 reshape.172
  27.6 18.0 %fusion.30 = (f32[2240]{0:T(1024)S(1)}, f32[2240,1,4,128]{3,2,1,0:T(4,128)}) fusion(bf16[2240,1,4,128]{3,2,1,0:T(4,128)(2,1)S(1)} %copy-done.2), kind=kLoop, calls=%fused_computation.59 | loop fusion | flops 3438400 | bytes 6890240 | tf_op jit(solution)/shard_map/reduce_sum | solution.py:55
  45.5 6.3 %reshape.164 = f32[70,32,512]{2,1,0:T(8,128)} reshape(f32[2240,1,4,128]{3,2,1,0:T(4,128)} %get-tuple-element.26) | data formatting | bytes 9175040 | tf_op jit(solution)/shard_map/reshape | solution.py:52
  51.9 0.8 slice_reduce_fusion.8
  52.7 4.6 convert_maximum_fusion
  57.3 6.3 %reshape.168 = f32[70,32,512]{2,1,0:T(8,128)} reshape(f32[2240,1,4,128]{3,2,1,0:T(4,128)} %convert_maximum_fusion) | data formatting | bytes 9175040 | tf_op jit(solution)/shard_map/reshape | solution.py:53
  63.6 0.1 reduce_sum.21
  63.7 65.3 %psum.29 = f32[70,32]{1,0:T(8,128)S(1)} all-reduce(f32[70,32]{1,0:T(8,128)S(1)} %reduce_sum.21), channel_id=1, replica_groups=mesh['frame'=32,'row'=4] {'frame','row'}, use_global_device_ids=true, to_apply=%region_2.3 | all-reduce | flops 2240 | bytes 17920 | tf_op jit(solution)/shard_map/psum | solution.py:56
  129.1 4.8 fusion.33
  133.8 0.7 copy-done.5
  134.5 8.0 %fusion.29 = f32[70,32,32]{2,1,0:T(8,128)} fusion(f32[70,32,512]{2,1,0:T(8,128)S(1)} %copy-done, f32[70,32,512]{2,1,0:T(8,128)} %reshape.172, f32[70,512]{1,0:T(8,128)S(1)} %bitcast_add_fusion), kind=kOutput, calls=%fused_computation.56 | convolution fusion | flops 441548800 | bytes 9605120 | tf_op jit(solution)/shard_map/hjt,het->hje/dot_general | solution.py:66
  142.5 1.5 broadcast_compare_fusion.1
  144.1 5.7 %copy.25 = bf16[2240,1,1,128]{3,2,1,0:T(2,128)(2,1)S(1)} copy(bf16[2240,1,1,128]{3,0,2,1:T(8,128)(2,1)} %collective-permute-done.1) | data formatting | bytes 1146880 | tf_op jit(solution)/shard_map/ppermute | solution.py:18
  149.8 5.9 %copy.24 = bf16[2240,1,1,128]{3,2,1,0:T(2,128)(2,1)S(1)} copy(bf16[2240,1,1,128]{3,0,2,1:T(8,128)(2,1)} %collective-permute-done) | data formatting | bytes 1146880 | tf_op jit(solution)/shard_map/ppermute | solution.py:17
  155.8 3.6 maximum_convert_fusion
  159.5 41.7 %fusion.8 = f32[2240,1,4,128]{3,2,1,0:T(4,128)} fusion(f32[2240,1,6,128]{3,2,1,0:T(8,128)S(1)} %maximum_convert_fusion, f32[2240]{0:T(1024)S(1)} %get-tuple-element.13, f32[2240]{0:T(1024)S(1)} %get-tuple-element.14, f32[2240]{0:T(1024)S(1)} %get-tuple-element.15, f32[2240]{0:T(1024)S(1)} %get-tuple-element.16, f32[2240]{0:T(1024)S(1)} %get-tuple-element.17, ...), kind=kLoop, calls=%fused_computation.20 | loop fusion | flops 19496960 | bytes 27635712 | tf_op jit(solution)/shard_map/add | solution.py:33
  201.2 6.3 %reshape.165 = f32[70,32,512]{2,1,0:T(8,128)} reshape(f32[2240,1,4,128]{3,2,1,0:T(4,128)} %fusion.8) | data formatting | bytes 9175040 | tf_op jit(solution)/shard_map/reshape | solution.py:51
  207.5 9.0 %fusion.37 = f32[70,32,32]{2,1,0:T(8,128)} fusion(f32[70,32,512]{2,1,0:T(8,128)} %reshape.164, f32[70,32,512]{2,1,0:T(8,128)} %reshape.165), kind=kOutput, calls=%fused_computation.78 | convolution fusion | flops 440401920 | bytes 9461760 | tf_op jit(solution)/shard_map/hjt,het->hje/dot_general | solution.py:54
  216.5 0.0 all-reduce.5.cloned.1.call-update
  216.5 2.5 broadcast_compare_fusion
  219.0 3.3 gt.13
  222.3 4.8 gt.15
  227.1 138.8 %all-reduce.5.cloned.1.call-done = (f32[70,32,32]{2,1,0:T(8,128)}, f32[70,32,32]{2,1,0:T(8,128)}) async-done(((f32[70,32,32]{2,1,0:T(8,128)}, f32[70,32,32]{2,1,0:T(8,128)}), (f32[70,32,32]{2,1,0:T(8,128)}, f32[70,32,32]{2,1,0:T(8,128)})) %all-reduce.5.cloned.1.call-update) | async-done | bytes 573456 | tf_op jit(solution)/shard_map/psum | solution.py:56
  365.9 8.2 %multiply_reduce_fusion = f32[70,512]{1,0:T(8,128)S(1)} fusion(f32[70,32,512]{2,1,0:T(8,128)} %reshape.172, f32[70,32,32]{2,1,0:T(8,128)} %get-tuple-element.21, f32[70,32,512]{2,1,0:T(8,128)} %reshape.168, f32[70,512]{1,0:T(8,128)S(1)} %copy-done.10), kind=kOutput, calls=%fused_computation.50 | convolution fusion | flops 443806720 | bytes 9748480 | tf_op jit(solution)/shard_map/hje,hjt->het/dot_general | solution.py:61
  374.1 0.7 negate_divide_fusion
  374.9 5.2 convolution_convert_fusion
  380.0 4.1 convert_element_type.73
  384.2 1.7 fusion.35
  385.9 0.9 copy.44
  386.8 2.9 collective-permute-start.3
  389.7 0.9 copy.43
  390.6 4.4 collective-permute-start.2
  395.1 8.6 %select_convert_fusion.1 = bf16[70,32,512]{2,1,0:T(8,128)(2,1)} fusion(pred[70,32,512]{2,1,0:T(32,128)(4,1)S(1)} %copy-done.7, f32[70,512]{1,0:T(8,128)S(1)} %copy-done.8, f32[70,32]{1,0:T(8,128)S(1)} %psum.29, f32[70,32,32]{2,1,0:T(8,128)S(1)} %copy-done.25, f32[70,32,512]{2,1,0:T(8,128)} %reshape.172, f32[70,512]{1,0:T(8,128)S(1)} %copy-done.11), kind=kOutput, calls=%fused_computation.49 | convolution fusion | flops 446136320 | bytes 8610560 | tf_op jit(solution)/shard_map/hje,het->hjt/dot_general | solution.py:70
  403.7 4.1 fusion.31
  407.7 5.1 reshape.169
  412.9 64.3 %psum.31 = f32[70,32]{1,0:T(8,128)S(1)} all-reduce(f32[70,32]{1,0:T(8,128)S(1)} %bitcast.32), channel_id=1, replica_groups=mesh['frame'=32,'row'=4] {'frame','row'}, use_global_device_ids=true, to_apply=%region_5.6 | all-reduce | flops 2240 | bytes 17920 | tf_op jit(solution)/shard_map/psum | solution.py:68
  477.2 8.6 %select_convert_fusion = bf16[70,32,512]{2,1,0:T(8,128)(2,1)} fusion(pred[70,32,512]{2,1,0:T(32,128)(4,1)S(1)} %gt.15, f32[70,32]{1,0:T(8,128)S(1)} %psum.31, f32[70,32,32]{2,1,0:T(8,128)} %get-tuple-element.22, f32[70,32,512]{2,1,0:T(8,128)} %reshape.165), kind=kOutput, calls=%fused_computation.48 | convolution fusion | flops 443842560 | bytes 8323840 | tf_op jit(solution)/shard_map/hje,het->hjt/dot_general | solution.py:80
  485.8 5.1 reshape.170
  490.9 5.7 %copy.32 = bf16[2240,1,1,128]{3,2,1,0:T(2,128)(2,1)S(1)} copy(bf16[2240,1,1,128]{3,0,2,1:T(8,128)(2,1)} %collective-permute-done.3) | data formatting | bytes 1146880 | tf_op jit(solution)/shard_map/ppermute | solution.py:18
  496.7 5.7 %copy.30 = bf16[2240,1,1,128]{3,2,1,0:T(2,128)(2,1)S(1)} copy(bf16[2240,1,1,128]{3,0,2,1:T(8,128)(2,1)} %collective-permute-done.2) | data formatting | bytes 1146880 | tf_op jit(solution)/shard_map/ppermute | solution.py:17
  502.5 3.6 maximum_convert_fusion.1
  506.2 41.7 %fusion.28 = bf16[2240,1,4,128]{3,2,1,0:T(4,128)(2,1)} fusion(f32[2240,1,6,128]{3,2,1,0:T(8,128)S(1)} %maximum_convert_fusion.1, f32[2240]{0:T(1024)S(1)} %get-tuple-element.13, f32[2240]{0:T(1024)S(1)} %get-tuple-element.14, f32[2240]{0:T(1024)S(1)} %copy-done.13, f32[2240]{0:T(1024)S(1)} %copy-done.15, f32[2240]{0:T(1024)S(1)} %copy-done.17, ...), kind=kLoop, calls=%fused_computation.53 | loop fusion | flops 20643840 | bytes 25341952 | tf_op jit(solution)/shard_map/convert_element_type | solution.py:89
  (68 shorter events, 0.2 us)
Async XLA Ops:
  7.2 358.7 %all-reduce.5.cloned.1.call-start = ((), (), s32[]{:S(2)}) async-start(), calls=%async_computation | async-start | bytes 4587520 | tf_op jit(solution)/shard_map/psum | solution.py:56
  12.6 14.9 %copy-start.2 = (bf16[2240,1,4,128]{3,2,1,0:T(4,128)(2,1)S(1)}, bf16[2240,1,4,128]{3,2,1,0:T(4,128)(2,1)}, u32[]{:S(2)}) copy-start(bf16[2240,1,4,128]{3,2,1,0:T(4,128)(2,1)} %param.6) | copy-start | bytes 6881284
  12.6 131.5 %collective-permute-start.1 = (bf16[2240,1,1,128]{3,0,2,1:T(8,128)(2,1)}, bf16[2240,1,1,128]{3,0,2,1:T(8,128)(2,1)}, u32[]{:S(2)}, u32[]{:S(2)}) collective-permute-start(bf16[2240,1,1,128]{3,0,2,1:T(8,128)(2,1)} %copy.42), channel_id=1, source_target_pairs={{1,0},{2,1},{3,2},{5,4},{6,5},{7,6},{9,8},{10,9},{11,10},{13,12},{... | collective-permute-start | bytes 1720328 | tf_op jit(solution)/shard_map/ppermute | solution.py:18
  16.9 132.9 %collective-permute-start = (bf16[2240,1,1,128]{3,0,2,1:T(8,128)(2,1)}, bf16[2240,1,1,128]{3,0,2,1:T(8,128)(2,1)}, u32[]{:S(2)}, u32[]{:S(2)}) collective-permute-start(bf16[2240,1,1,128]{3,0,2,1:T(8,128)(2,1)} %copy.41), channel_id=1, source_target_pairs={{0,1},{1,2},{2,3},{4,5},{5,6},{6,7},{8,9},{9,10},{10,11},{12,13},{... | collective-permute-start | bytes 1720328 | tf_op jit(solution)/shard_map/ppermute | solution.py:17
  45.5 6.3 %copy-start.24 = (bf16[3,3,2240]{2,1,0:T(4,128)(2,1)S(1)}, bf16[3,3,2240]{2,1,0:T(4,128)(2,1)}, u32[]{:S(2)}) copy-start(bf16[3,3,2240]{2,1,0:T(4,128)(2,1)} %param.9) | copy-start | bytes 120964
  52.7 106.8 %copy-start.12 = (f32[2240]{0:T(1024)}, f32[2240]{0:T(1024)S(1)}, u32[]{:S(2)}) copy-start(f32[2240]{0:T(1024)S(1)} %get-tuple-element.15) | copy-start | bytes 26884
  52.7 106.8 %copy-start.14 = (f32[2240]{0:T(1024)}, f32[2240]{0:T(1024)S(1)}, u32[]{:S(2)}) copy-start(f32[2240]{0:T(1024)S(1)} %get-tuple-element.16) | copy-start | bytes 26884
  52.7 106.8 %copy-start.16 = (f32[2240]{0:T(1024)}, f32[2240]{0:T(1024)S(1)}, u32[]{:S(2)}) copy-start(f32[2240]{0:T(1024)S(1)} %get-tuple-element.17) | copy-start | bytes 26884
  129.1 5.5 copy-start
  133.8 0.7 copy-start.5
  134.5 8.0 %copy-start.9 = (f32[70,512]{1,0:T(8,128)}, f32[70,512]{1,0:T(8,128)S(1)}, u32[]{:S(2)}) copy-start(f32[70,512]{1,0:T(8,128)S(1)} %bitcast_add_fusion) | copy-start | bytes 430084
  134.5 8.0 %copy-start.3 = (bf16[2240,1,4,128]{3,2,1,0:T(4,128)(2,1)S(1)}, bf16[2240,1,4,128]{3,2,1,0:T(4,128)(2,1)}, u32[]{:S(2)}) copy-start(bf16[2240,1,4,128]{3,2,1,0:T(4,128)(2,1)} %param.5) | copy-start | bytes 6881284
  142.5 13.2 %copy-start.1 = (bf16[2240,1,4,128]{3,2,1,0:T(4,128)(2,1)S(1)}, bf16[2240,1,4,128]{3,2,1,0:T(4,128)(2,1)}, u32[]{:S(2)}) copy-start(bf16[2240,1,4,128]{3,2,1,0:T(4,128)(2,1)} %param.7) | copy-start | bytes 6881284
  155.8 3.7 copy-start.18
  155.8 3.7 copy-start.20
  155.8 3.7 copy-start.22
  219.0 146.9 %copy-start.10 = (f32[70,512]{1,0:T(8,128)S(1)}, f32[70,512]{1,0:T(8,128)}, u32[]{:S(2)}) copy-start(f32[70,512]{1,0:T(8,128)} %copy-done.9) | copy-start | bytes 430084
  222.3 152.6 %slice-start.2 = ((s8[4587520]{0:T(1024)(128)(4,1)}), s8[393216]{0:T(1024)(128)(4,1)S(1)}, s32[]{:S(2)}) async-start(s8[4587520]{0:T(1024)(128)(4,1)} %bitcast.26), calls=%async_computation.3 | async-start | bytes 786432
  365.9 8.2 %copy-start.6 = (f32[70,1,512]{2,1,0:T(1,128)S(1)}, f32[70,1,512]{2,1,0:T(1,128)}, u32[]{:S(2)}) copy-start(f32[70,1,512]{2,1,0:T(1,128)} %copy-done.5) | copy-start | bytes 430084
  365.9 8.9 %slice-start.3 = ((s8[4587520]{0:T(1024)(128)(4,1)}), s8[4194304]{0:T(1024)(128)(4,1)S(1)}, s32[]{:S(2)}) async-start(s8[4587520]{0:T(1024)(128)(4,1)} %bitcast.26), calls=%async_computation.4 | async-start | bytes 8388608
  365.9 8.9 %copy-start.4 = (f32[70,32,32]{2,1,0:T(8,128)S(1)}, f32[70,32,32]{2,1,0:T(8,128)}, u32[]{:S(2)}) copy-start(f32[70,32,32]{2,1,0:T(8,128)} %get-tuple-element.22) | copy-start | bytes 860164
  384.2 10.9 %copy-start.7 = (pred[70,32,512]{2,1,0:T(32,128)(4,1)S(1)}, pred[70,32,512]{2,1,0:T(32,128)(4,1)}, u32[]{:S(2)}) copy-start(pred[70,32,512]{2,1,0:T(32,128)(4,1)} %gt.13) | copy-start | bytes 3440644
  384.2 10.9 %copy-start.8 = (f32[70,512]{1,0:T(8,128)S(1)}, f32[70,512]{1,0:T(8,128)}, u32[]{:S(2)}) copy-start(f32[70,512]{1,0:T(8,128)} %negate_divide_fusion) | copy-start | bytes 430084
  384.2 10.9 %copy-start.11 = (f32[70,512]{1,0:T(8,128)S(1)}, f32[70,512]{1,0:T(8,128)}, u32[]{:S(2)}) copy-start(f32[70,512]{1,0:T(8,128)} %copy-done.9) | copy-start | bytes 430084
  384.2 10.9 %copy-start.25 = (f32[70,32,32]{2,1,0:T(8,128)S(1)}, f32[70,32,32]{2,1,0:T(8,128)}, u32[]{:S(2)}) copy-start(f32[70,32,32]{2,1,0:T(8,128)} %get-tuple-element.21) | copy-start | bytes 860164
  386.8 104.2 %collective-permute-start.3 = (bf16[2240,1,1,128]{3,0,2,1:T(8,128)(2,1)}, bf16[2240,1,1,128]{3,0,2,1:T(8,128)(2,1)}, u32[]{:S(2)}, u32[]{:S(2)}) collective-permute-start(bf16[2240,1,1,128]{3,0,2,1:T(8,128)(2,1)} %copy.44), channel_id=1, source_target_pairs={{1,0},{2,1},{3,2},{5,4},{6,5},{7,6},{9,8},{10,9},{11,10},{13,12},{... | collective-permute-start | bytes 1720328 | tf_op jit(solution)/shard_map/ppermute | solution.py:18
  389.7 13.9 %slice-start = ((s8[4587520]{0:T(1024)(128)(4,1)}), s8[4194304]{0:T(1024)(128)(4,1)S(1)}, s32[]{:S(2)}) async-start(s8[4587520]{0:T(1024)(128)(4,1)} %bitcast.24), calls=%async_computation.1 | async-start | bytes 8388608
  390.6 13.0 %slice-start.1 = ((s8[4587520]{0:T(1024)(128)(4,1)}), s8[393216]{0:T(1024)(128)(4,1)S(1)}, s32[]{:S(2)}) async-start(s8[4587520]{0:T(1024)(128)(4,1)} %bitcast.24), calls=%async_computation.2 | async-start | bytes 786432
  390.6 106.1 %collective-permute-start.2 = (bf16[2240,1,1,128]{3,0,2,1:T(8,128)(2,1)}, bf16[2240,1,1,128]{3,0,2,1:T(8,128)(2,1)}, u32[]{:S(2)}, u32[]{:S(2)}) collective-permute-start(bf16[2240,1,1,128]{3,0,2,1:T(8,128)(2,1)} %copy.43), channel_id=1, source_target_pairs={{0,1},{1,2},{2,3},{4,5},{5,6},{6,7},{8,9},{9,10},{10,11},{12,13},{... | collective-permute-start | bytes 1720328 | tf_op jit(solution)/shard_map/ppermute | solution.py:17
  502.4 3.7 copy-start.13
  502.4 3.7 copy-start.15
  502.4 3.7 copy-start.17
  502.4 3.7 copy-start.19
  502.4 3.7 copy-start.21
  502.5 3.7 copy-start.23
Sparse Core Ops, SparseCore 0:
  216.6 149.2 all-reduce.4
where the time goes:
time: 562 us; the launch traced here: 555 us
  waiting for transfers between devices  139 us (25%)
  blocking collectives  130 us (23%)
  other arithmetic  118 us (21%)
  local copies, waits for them, and re-layouts  81 us (14%)
  matrix products  56.3 us (10%)
  starting transfers between devices  16.3 us (3%)
  between operations  14.7 us (3%)
    psum x1, waiting for transfers between devices, shards(): state, key_sum = lax.psum((local_state, local_sum), ('frame', 'row'))  139 us
    psum x1, blocking collectives, shards(): state, key_sum = lax.psum((local_state, local_sum), ('frame', 'row'))  65.3 us
    psum x1, blocking collectives, shards(): lax.psum((local_gstate, local_gsum), ('frame', 'row'))  64.3 us
    convert_element_type x1, other arithmetic, shards(): conv_taps(pad_columns(grad_ext), weights, True, row_count, col_count)  41.7 us
    add x1, other arithmetic, conv_taps(): summed = tap_term if summed is None else summed + tap_term  41.7 us
    reduce_sum x1, other arithmetic, shards(): local_sum = jnp.sum(key_act, axis=2)  18 us
    ppermute x2, local copies, waits for them, and re-layouts, extended(): before = lax.ppermute(last, axis, up)  11.7 us
    ppermute x2, local copies, waits for them, and re-layouts, extended(): after = lax.ppermute(leading, axis, down)  11.4 us
  transfers between devices with their start and end apart: 5, of which 1 were waited for; matrix products, arithmetic and copies ran while one was open for 20% of the time, Pallas kernels for 0%

commit v1 on v0

--- a/solution.py
+++ b/solution.py
@@ -65,7 +65,7 @@
     grad_den = -jnp.sum(grad_out * output, axis=1) / denom
     local_gstate = jnp.einsum("hjt,het->hje", query_act, grad_num, precision=highest)
     local_gsum = jnp.einsum("hjt,ht->hj", query_act, grad_den, precision=highest)
-    grad_state, grad_sum = lax.psum((local_gstate, local_gsum), ("frame", "row"))
+    grad_state, grad_sum = lax.psum(lax.psum((local_gstate, local_gsum), "row"), "frame")
     grad_qact = (
         jnp.einsum("hje,het->hjt", state, grad_num, precision=highest)
         + key_sum[:, :, None] * grad_den[:, None, :]

time: 562 us -> 971 us (1.73)
  the two profiles are of different devices: /device:TPU:1 before, /device:TPU:0 now
where the time goes in v1:
time: 971 us; the launch traced here: 966 us
  waiting for transfers between devices  474 us (49%)
  blocking collectives  239 us (25%)
  other arithmetic  97.2 us (10%)
  local copies, waits for them, and re-layouts  75.7 us (8%)
  matrix products  58.4 us (6%)
  between operations  14.3 us (1%)
    psum x1, waiting for transfers between devices, shards(): lax.psum(lax.psum((local_gstate, local_gsum), 'row'), 'frame')  292 us
    psum x1, blocking collectives, shards(): lax.psum(lax.psum((local_gstate, local_gsum), 'row'), 'frame')  155 us
    psum x1, waiting for transfers between devices, shards(): state, key_sum = lax.psum((local_state, local_sum), ('frame', 'row'))  140 us
    psum x1, blocking collectives, shards(): state, key_sum = lax.psum((local_state, local_sum), ('frame', 'row'))  68.6 us
    convert_element_type x1, other arithmetic, shards(): conv_taps(pad_columns(grad_ext), weights, True, row_count, col_count)  61.2 us
    psum x1, waiting for transfers between devices, shards(): lax.psum((local_gstate, local_gsum), 'row')  42.4 us
  transfers between devices with their start and end apart: 7, of which 3 were waited for; matrix products, arithmetic and copies ran while one was open for 6% of the time, Pallas kernels for 0%

profile of v1, /device:TPU:0, one launch (start us, length us, event | category | flops | bytes accessed | tf_op | source)
XLA Modules:
  0.0 966.2 jit_solution(356597379997661655)
XLA Ops:
  7.2 4.6 convert_maximum_fusion
  11.8 6.5 reshape.168
  18.3 17.9 %fusion.30 = (f32[2240]{0:T(1024)S(1)}, f32[2240,1,4,128]{3,2,1,0:T(4,128)}) fusion(bf16[2240,1,4,128]{3,2,1,0:T(4,128)(2,1)S(1)} %copy-done), kind=kLoop, calls=%fused_computation.59 | loop fusion | flops 3438400 | bytes 6890240 | tf_op jit(solution)/shard_map/reduce_sum | solution.py:55
  36.2 0.1 reduce_sum.21
  36.2 68.6 %psum.43 = f32[70,32]{1,0:T(8,128)S(1)} all-reduce(f32[70,32]{1,0:T(8,128)S(1)} %reduce_sum.21), channel_id=1, replica_groups=mesh['frame'=32,'row'=4] {'frame','row'}, use_global_device_ids=true, to_apply=%region_2.3 | all-reduce | flops 2240 | bytes 17920 | tf_op jit(solution)/shard_map/psum | solution.py:56
  104.9 4.6 fusion.33
  109.5 0.6 copy-done.7
  110.2 2.8 reshape.172
  113.0 9.3 fusion.29
  122.3 0.0 all-reduce.10.cloned.1.call-start
  122.4 42.4 %all-reduce.8.cloned.1.call-done = f32[70,32,32]{2,1,0:T(8,128)} async-done(((f32[70,32,32]{2,1,0:T(8,128)}), f32[70,32,32]{2,1,0:T(8,128)}) %all-reduce.8.cloned.1.call-update) | async-done | bytes 286736 | tf_op jit(solution)/shard_map/psum | solution.py:68
  164.9 1.7 fusion.36
  166.6 0.9 copy.41
  167.4 3.1 collective-permute-start
  170.5 0.9 copy.42
  171.4 1.5 collective-permute-start.1
  172.9 6.3 reshape.164
  179.2 291.7 %all-reduce.10.cloned.1.call-done = f32[70,32,32]{2,1,0:T(8,128)} async-done(((f32[70,32,32]{2,1,0:T(8,128)}), f32[70,32,32]{2,1,0:T(8,128)}) %all-reduce.10.cloned.1.call-update) | async-done | bytes 286736 | tf_op jit(solution)/shard_map/psum | solution.py:68
  471.0 7.2 convolution_convert_fusion
  478.2 4.1 convert_element_type.73
  482.3 1.7 fusion.35
  484.0 0.1 copy.43
  484.1 1.5 collective-permute-start.2
  485.5 0.1 copy.44
  485.6 1.3 collective-permute-start.3
  486.9 1.5 broadcast_compare_fusion
  488.5 0.2 slice_reduce_fusion.8
  488.8 5.7 copy.24
  494.5 5.7 copy.25
  500.2 3.6 maximum_convert_fusion
  503.9 9.3 copy.30
  513.2 9.3 copy.32
  522.5 5.7 maximum_convert_fusion.1
  528.2 61.2 %fusion.28 = (bf16[2240,1,4,128]{3,2,1,0:T(4,128)(2,1)}, f32[2240,1,4,128]{3,2,1,0:T(4,128)}) fusion(f32[2240,1,6,128]{3,2,1,0:T(8,128)} %maximum_convert_fusion.1, f32[2240]{0:T(1024)S(1)} %get-tuple-element.13, f32[2240]{0:T(1024)S(1)} %get-tuple-element.14, f32[2240]{0:T(1024)S(1)} %get-tuple-element.15, f32[2240]{0:T(1024)S(1)} %get-tuple-element.16, ...), kind=kLoop, calls=%fused_computation.53 | loop fusion | flops 40140800 | bytes 52867072 | tf_op jit(solution)/shard_map/convert_element_type | solution.py:89
  589.4 6.7 reshape.165
  596.2 9.1 fusion.37
  605.3 2.5 broadcast_compare_fusion.1
  607.8 3.3 gt.15
  611.1 5.6 gt.13
  616.7 140.1 %all-reduce.6.cloned.1.call-done = f32[70,32,32]{2,1,0:T(8,128)} async-done(((f32[70,32,32]{2,1,0:T(8,128)}), f32[70,32,32]{2,1,0:T(8,128)}) %all-reduce.6.cloned.1.call-update) | async-done | bytes 286736 | tf_op jit(solution)/shard_map/psum | solution.py:56
  756.8 7.6 multiply_reduce_fusion
  764.5 5.9 fusion.31
  770.4 15.3 %psum.46 = f32[70,32]{1,0:T(8,128)S(1)} all-reduce(f32[70,32]{1,0:T(8,128)S(1)} %bitcast.28), channel_id=1, replica_groups=mesh['frame'=32,'row'=4] {'row'}, use_global_device_ids=true, to_apply=%region_6.7 | all-reduce | flops 2240 | bytes 17920 | tf_op jit(solution)/shard_map/psum | solution.py:68
  785.7 154.9 %psum.47 = f32[70,32]{1,0:T(8,128)S(1)} all-reduce(f32[70,32]{1,0:T(8,128)S(1)} %psum.46), channel_id=1, replica_groups=mesh['frame'=32,'row'=4] {'frame'}, use_global_device_ids=true, to_apply=%region_7.8 | all-reduce | flops 2240 | bytes 17920 | tf_op jit(solution)/shard_map/psum | solution.py:68
  940.6 7.2 select_convert_fusion
  947.8 2.1 reshape.170
  949.9 7.5 select_convert_fusion.1
  957.3 2.1 reshape.169
  (40 shorter events, 0.3 us)
Async XLA Ops:
  7.2 157.6 %all-reduce.8.cloned.1.call-start = ((), (), s32[]{:S(2)}) async-start(), calls=%async_computation.1 | async-start | bytes 2293760 | tf_op jit(solution)/shard_map/psum | solution.py:68
  11.8 6.5 copy-start
  36.2 74.0 %copy-start.6 = (bf16[2240,1,4,128]{3,2,1,0:T(4,128)(2,1)S(1)}, bf16[2240,1,4,128]{3,2,1,0:T(4,128)(2,1)}, u32[]{:S(2)}) copy-start(bf16[2240,1,4,128]{3,2,1,0:T(4,128)(2,1)} %param.8) | copy-start | bytes 6881284
  109.5 0.6 copy-start.7
  110.2 12.1 %copy-start.11 = (f32[70,512]{1,0:T(8,128)}, f32[70,512]{1,0:T(8,128)S(1)}, u32[]{:S(2)}) copy-start(f32[70,512]{1,0:T(8,128)S(1)} %bitcast_add_fusion) | copy-start | bytes 430084
  113.0 51.9 %copy-start.2 = (bf16[2240,1,4,128]{3,2,1,0:T(4,128)(2,1)S(1)}, bf16[2240,1,4,128]{3,2,1,0:T(4,128)(2,1)}, u32[]{:S(2)}) copy-start(bf16[2240,1,4,128]{3,2,1,0:T(4,128)(2,1)} %param.7) | copy-start | bytes 6881284
  122.3 348.6 %all-reduce.10.cloned.1.call-start = ((), (), s32[]{:S(2)}) async-start(), calls=%async_computation.2 | async-start | bytes 2293760 | tf_op jit(solution)/shard_map/psum | solution.py:68
  164.8 592.0 %all-reduce.6.cloned.1.call-start = ((), (), s32[]{:S(2)}) async-start(), calls=%async_computation | async-start | bytes 2293760 | tf_op jit(solution)/shard_map/psum | solution.py:56
  167.4 321.3 %collective-permute-start = (bf16[2240,1,1,128]{3,0,2,1:T(8,128)(2,1)}, bf16[2240,1,1,128]{3,0,2,1:T(8,128)(2,1)}, u32[]{:S(2)}, u32[]{:S(2)}) collective-permute-start(bf16[2240,1,1,128]{3,0,2,1:T(8,128)(2,1)} %copy.41), channel_id=1, source_target_pairs={{0,1},{1,2},{2,3},{4,5},{5,6},{6,7},{8,9},{9,10},{10,11},{12,13},{... | collective-permute-start | bytes 1720328 | tf_op jit(solution)/shard_map/ppermute | solution.py:17
  171.4 323.0 %collective-permute-start.1 = (bf16[2240,1,1,128]{3,0,2,1:T(8,128)(2,1)}, bf16[2240,1,1,128]{3,0,2,1:T(8,128)(2,1)}, u32[]{:S(2)}, u32[]{:S(2)}) collective-permute-start(bf16[2240,1,1,128]{3,0,2,1:T(8,128)(2,1)} %copy.42), channel_id=1, source_target_pairs={{1,0},{2,1},{3,2},{5,4},{6,5},{7,6},{9,8},{10,9},{11,10},{13,12},{... | collective-permute-start | bytes 1720328 | tf_op jit(solution)/shard_map/ppermute | solution.py:18
  482.3 4.6 copy-start.1
  484.0 4.5 copy-start.13
  484.1 16.2 %copy-start.3 = (bf16[2240,1,4,128]{3,2,1,0:T(4,128)(2,1)S(1)}, bf16[2240,1,4,128]{3,2,1,0:T(4,128)(2,1)}, u32[]{:S(2)}) copy-start(bf16[2240,1,4,128]{3,2,1,0:T(4,128)(2,1)} %param.7) | copy-start | bytes 6881284
  484.1 19.8 %collective-permute-start.2 = (bf16[2240,1,1,128]{3,0,2,1:T(8,128)(2,1)S(1)}, bf16[2240,1,1,128]{3,0,2,1:T(8,128)(2,1)S(1)}, u32[]{:S(2)}, u32[]{:S(2)}) collective-permute-start(bf16[2240,1,1,128]{3,0,2,1:T(8,128)(2,1)S(1)} %copy.43), channel_id=1, source_target_pairs={{0,1},{1,2},{2,3},{4,5},{5,6},{6,7},{8,9},{9,10},{10,11},{12,13},{... | collective-permute-start | bytes 1720328 | tf_op jit(solution)/shard_map/ppermute | solution.py:17
  485.6 27.5 %collective-permute-start.3 = (bf16[2240,1,1,128]{3,0,2,1:T(8,128)(2,1)S(1)}, bf16[2240,1,1,128]{3,0,2,1:T(8,128)(2,1)S(1)}, u32[]{:S(2)}, u32[]{:S(2)}) collective-permute-start(bf16[2240,1,1,128]{3,0,2,1:T(8,128)(2,1)S(1)} %copy.44), channel_id=1, source_target_pairs={{1,0},{2,1},{3,2},{5,4},{6,5},{7,6},{9,8},{10,9},{11,10},{13,12},{... | collective-permute-start | bytes 1720328 | tf_op jit(solution)/shard_map/ppermute | solution.py:18
  596.1 9.1 copy-start.4
  607.8 149.0 %copy-start.12 = (f32[70,512]{1,0:T(8,128)S(1)}, f32[70,512]{1,0:T(8,128)}, u32[]{:S(2)}) copy-start(f32[70,512]{1,0:T(8,128)} %copy-done.11) | copy-start | bytes 430084
  616.7 147.7 %copy-start.8 = (f32[70,1,512]{2,1,0:T(1,128)S(1)}, f32[70,1,512]{2,1,0:T(1,128)}, u32[]{:S(2)}) copy-start(f32[70,1,512]{2,1,0:T(1,128)} %copy-done.7) | copy-start | bytes 430084
  764.4 176.2 %copy-start.5 = (pred[70,32,512]{2,1,0:T(32,128)(4,1)S(1)}, pred[70,32,512]{2,1,0:T(32,128)(4,1)}, u32[]{:S(2)}) copy-start(pred[70,32,512]{2,1,0:T(32,128)(4,1)} %gt.15) | copy-start | bytes 3440644
  764.5 21.2 %copy-start.10 = (f32[70,512]{1,0:T(8,128)}, f32[70,512]{1,0:T(8,128)S(1)}, u32[]{:S(2)}) copy-start(f32[70,512]{1,0:T(8,128)S(1)} %negate_divide_fusion) | copy-start | bytes 430084
  947.8 2.1 copy-start.9
Sparse Core Ops, SparseCore 0:
  122.4 42.3 all-reduce.7
  167.3 303.6 all-reduce.9
  605.4 151.3 all-reduce.5
